TPU v7x, 32 devices: a whole 2x2x4 slice. The times are simulated.
32 devices in a mesh: groups: 2 (over y), loans: 4 (over z), paths: 4 (over x, core).
Axes of the slice: x: 2, y: 2, z: 4, core: 2. Of those that a mesh axis runs over, the one named last changes fastest.
Arguments:
- loan_features: bfloat16 [8192, 128], P(('groups', 'loans')), parts along dimension 0, may hold values from -6 to 6
- hazard_coef: bfloat16 [128, 2], replicated, may hold values from -0.5 to 0.5
- coupon: float32 [8192], P(('groups', 'loans')), parts along dimension 0, may hold values from 0.03 to 0.075
- balance: float32 [8192], P(('groups', 'loans')), parts along dimension 0, may hold values from 0.25 to 4
- loan_term: int32 [8192], P(('groups', 'loans')), parts along dimension 0, may hold values from 180 to 360
- loan_age: int32 [8192], P(('groups', 'loans')), parts along dimension 0, may hold values from 0 to 119
- loan_region: int32 [8192], P(('groups', 'loans')), parts along dimension 0, may hold values from 0 to 415
- loan_deal: int32 [8192], P(('groups', 'loans')), parts along dimension 0, may hold values from 0 to 31, as said below
- region_hpi: float32 [832, 6, 512], P(('groups', 'loans'), None, 'paths'), parts along dimension 0, may hold values from -0.6 to 0.6
- rate_paths: float32 [2, 6, 1024], P(None, None, ('groups', 'paths')), parts along dimension 2, may hold values from 0.01 to 0.08
- deal_owner: int32 [64, 1], P('groups'), parts along dimension 0, may hold values from 0 to 3; in each aligned block of 32 rows (0 to 31, 32 to 63, ...) at most 24 rows name the same one
- tranche_order: int32 [64, 64], P('groups'), parts along dimension 0, may hold values from 0 to 63, each once within a row
- tranche_share: float32 [64, 64], P('groups'), parts along dimension 0, may hold values from 0.2 to 5
- tranche_rate: float32 [64, 64], P('groups'), parts along dimension 0, may hold values from 0.02 to 0.07
Outputs:
- tranche_value: float32 [64, 64], P('groups'), parts along dimension 0
There are 2 independent parts, one for each index of `groups`. A program takes and returns all parts, laid end to end along the dimension named above; an argument that names none is the same for every part. Nothing has to cross between parts.
Inputs may be any that keep to these rules, and one draw needn't show every extreme that they name: `loan_deal`: every deal holds at least one loan. `deal_owner`: no index of loans owns more than 24 deals, and one owns exactly 24. `tranche_order`: each row names every tranche once.
All inputs are finite; a program needn't handle non-finite values.
Results may differ from a plain program's by a relative error of at most 0.0003.
Values sent between devices are 32-bit elements; how exact they have to be, the bound alone decides.
A program may use at most 64 MiB of HBM per device.

v0:
```python
import jax
import jax.numpy as jnp
from jax import lax
from jax.sharding import PartitionSpec as P

prepay_base = -4.0
incentive = 40.0
default_base = -6.0
price_sens = 12.0
oas_spread = 0.005


def loan_month(held, covar, coupon, rate_month, sched_rate, mortgage_now, hpi_now):
    smm = jax.nn.sigmoid(
        covar[:, 0][None, :] + prepay_base + incentive * (coupon[None, :] - mortgage_now[:, None])
    )
    mdr = jax.nn.sigmoid(covar[:, 1][None, :] + default_base - price_sens * hpi_now)
    interest = held * rate_month[None, :]
    sched = held * sched_rate[None, :]
    lost = mdr * held
    prepaid = smm * (held - sched - lost)
    principal = sched + prepaid + lost
    return (held - principal, principal, interest)


def priority_mask(tranche_order):
    count = tranche_order.shape[1]
    spots = jnp.arange(count, dtype=jnp.int32)
    hits = tranche_order[:, :, None] == spots[None, None, :]
    prio = jnp.sum(jnp.where(hits, spots[None, :, None], 0), axis=1)
    return (prio[:, :, None] < prio[:, None, :]).astype(jnp.float32)


def waterfall(princ, inter, starts, shares, rates, ahead_mask, short, valid):
    steps = princ.shape[2]
    blank = 1.0 - valid
    weights = shares / (jnp.sum(shares, axis=1, keepdims=True) + blank[:, None])
    opening = weights * starts[:, None]
    safe_open = opening + blank[:, None]
    held = jnp.broadcast_to(opening[:, None, :], (princ.shape[0], princ.shape[1], shares.shape[1]))
    decay = jnp.exp(-jnp.cumsum(short + oas_spread, axis=0) / 12.0)
    worth = jnp.zeros_like(held)
    for step in range(steps):
        ahead = jnp.einsum("xpj,xjk->xpk", held, ahead_mask, precision=lax.Precision.HIGHEST)
        paid = jnp.minimum(jnp.maximum(princ[:, :, step, None] - ahead, 0.0), held)
        coupon_due = rates[:, None, :] * held
        denom = jnp.sum(coupon_due, axis=2, keepdims=True) + blank[:, None, None]
        flow = paid + inter[:, :, step, None] * coupon_due / denom
        worth = worth + flow * decay[step][None, :, None]
        held = held - paid
    worth = worth + held * decay[steps - 1][None, :, None]
    return jnp.sum(worth / safe_open[:, None, :], axis=1)


def on_device(
    loan_features,
    hazard_coef,
    coupon,
    balance,
    loan_term,
    loan_age,
    loan_region,
    loan_deal,
    region_hpi,
    rate_paths,
    deal_owner,
    tranche_order,
    tranche_share,
    tranche_rate,
):
    highest = lax.Precision.HIGHEST
    loans_here = coupon.shape[0]
    paths_here = rate_paths.shape[2]
    steps = rate_paths.shape[1]
    deals = deal_owner.shape[0]
    groups = lax.axis_size("loans")
    me_loan = lax.axis_index("loans")
    covar = jnp.dot(loan_features, hazard_coef, preferred_element_type=jnp.float32)
    piece = lax.all_gather(region_hpi, "loans", axis=0, tiled=True)
    rows = piece.shape[0]
    marks = (loan_region[None, :] == lax.iota(jnp.int32, rows)[:, None]).astype(jnp.float32)
    loan_hpi = jnp.einsum("rc,rl->cl", piece.reshape(rows, -1), marks, precision=highest)
    loan_hpi = loan_hpi.reshape(steps, paths_here, loans_here)
    rate_month = coupon / 12.0
    term_left = (loan_term - loan_age).astype(jnp.float32)
    held = jnp.broadcast_to(balance[None, :], (paths_here, loans_here))
    prin_list = []
    int_list = []
    for step in range(steps):
        sched_rate = rate_month / jnp.expm1((term_left - step) * jnp.log1p(rate_month))
        held, principal, interest = loan_month(
            held, covar, coupon, rate_month, sched_rate, rate_paths[1, step], loan_hpi[step]
        )
        prin_list.append(principal)
        int_list.append(interest)
    cash = jnp.stack([jnp.stack(prin_list, 1), jnp.stack(int_list, 1)], 1)
    deal_ids = lax.iota(jnp.int32, deals)
    match = loan_deal[:, None] == deal_ids[None, :]
    onehot_deal = match.astype(jnp.float32)
    totals = lax.psum(jnp.dot(balance, onehot_deal, precision=highest), "loans")
    owners = deal_owner[:, 0]
    order_key = owners * deals + deal_ids
    position = jnp.sum((order_key[None, :] < order_key[:, None]).astype(jnp.int32), axis=1)
    place = (position[None, :] == deal_ids[:, None]).astype(jnp.float32)
    ahead_mask = priority_mask(tranche_order)
    portion = paths_here // groups
    block = cash.reshape(-1, loans_here)
    path_flows = lax.psum_scatter(
        jnp.dot(block, onehot_deal, precision=highest).reshape(
            portion * lax.axis_size("loans"), 2, steps, deals
        ),
        "loans",
        scatter_dimension=0,
        tiled=True,
    )
    flows = path_flows.transpose(3, 0, 1, 2)
    short = lax.dynamic_slice_in_dim(rate_paths[0], me_loan * portion, portion, 1)
    by_deal = waterfall(
        flows[:, :, 0, :],
        flows[:, :, 1, :],
        totals,
        tranche_share,
        tranche_rate,
        ahead_mask,
        short,
        jnp.ones((deals,), jnp.float32),
    )
    ordered = jnp.dot(place, by_deal, precision=highest)
    mine = lax.psum(ordered, "loans")
    total = lax.psum(mine, "paths")
    all_paths = paths_here * lax.axis_size("paths")
    return 100.0 * (total / all_paths - 1.0)


def solution(mesh):
    in_specs = (
        P(("groups", "loans"), None),
        P(),
        P(("groups", "loans")),
        P(("groups", "loans")),
        P(("groups", "loans")),
        P(("groups", "loans")),
        P(("groups", "loans")),
        P(("groups", "loans")),
        P(("groups", "loans"), None, "paths"),
        P(None, None, ("groups", "paths")),
        P("groups", None),
        P("groups", None),
        P("groups", None),
        P("groups", None),
    )
    out_specs = P("groups", None)
    return jax.shard_map(
        on_device, mesh=mesh, in_specs=in_specs, out_specs=out_specs, check_vma=False
    )
```

profile of v0, /device:TPU:0, one launch (start us, length us, event | category | flops | bytes accessed | tf_op | source)
XLA Modules:
  0.0 136.8 jit_solution(10805481417194301331)
XLA Ops:
  6.5 0.7 all-gather.2.cloned.1.call-update
  7.3 0.7 add_bitcast_fusion
  8.6 0.7 slice.140
  9.6 0.8 slice_bitcast_fusion.20
  10.4 0.8 fusion.190
  11.3 0.7 exponential-minus-one_divide_fusion
  12.0 0.7 exponential-minus-one_divide_fusion.1
  13.0 30.7 %all-gather.2.cloned.1.call-done = f32[416,6,128]{2,0,1:T(8,128)} async-done(((f32[104,6,128]{2,0,1:T(8,128)}), f32[416,6,128]{2,0,1:T(8,128)}) %all-gather.2.cloned.1.call-update) | async-done | bytes 1277968 | tf_op jit(solution)/shard_map/all_gather | solution.py:79
  43.6 4.7 %convolution_bitcast_fusion = f32[768,1024]{0,1:T(8,128)S(1)} fusion(s32[1024]{0:T(1024)} %param.20, f32[416,6,128]{2,0,1:T(8,128)} %all-gather.2.cloned.1.call-done), kind=kOutput, calls=%fused_computation.21 | convolution fusion | flops 3926294528 | bytes 4427776 | tf_op jit(solution)/shard_map/rc,rl->cl/dot_general | solution.py:82
  48.3 1.1 bitcast_dynamic-update-slice_fusion.9
  49.4 1.0 bitcast_dynamic-update-slice_fusion.8
  50.4 1.2 bitcast_dynamic-update-slice_fusion.7
  51.6 1.1 bitcast_dynamic-update-slice_fusion.6
  52.8 1.6 %bitcast_dynamic-update-slice_fusion.5 = (f32[128,6,1024]{0,2,1:T(8,128)S(1)}, f32[128,1024]{0,1:T(8,128)S(1)}, f32[128,6,1024]{0,2,1:T(8,128)S(1)}) fusion(f32[128,6,1024]{0,2,1:T(8,128)S(1)} %get-tuple-element.22, f32[768,1024]{0,1:T(8,128)S(1)} %convolution_bitcast_fusion, f32[1024]{0:T(1024)S(1)} %bitcast.124, f32[128]{0:T(128)S(1)} %get-tuple-element.48, ...), kind=kLoop, calls=%fused_computation.138 | loop fusion | flops 7471104 | bytes 3700224
  54.6 1.1 fusion.116
  55.7 6.0 %fusion.5 = f32[128,2,6,32]{3,0,2,1:T(8,128)} fusion(f32[128,1,6,1024]{0,3,2,1:T(8,128)S(1)} %bitcast.112, f32[128,1,6,1024]{0,3,2,1:T(8,128)S(1)} %bitcast.113, s32[1024]{0:T(1024)S(1)} %copy-done.6), kind=kOutput, calls=%fused_computation.5 | convolution fusion | flops 605585408 | bytes 6492160 | tf_op jit(solution)/shard_map/dot_general | solution.py:109
  62.0 10.2 %psum.21 = f32[32]{0:T(128)S(1)} all-reduce(f32[32]{0:T(128)S(1)} %convolution_bitcast_fusion.1), channel_id=1, replica_groups=mesh['groups'=2,'loans'=4,'paths'=4] {'loans'}, use_global_device_ids=true, to_apply=%region_3.4 | all-reduce | flops 32 | bytes 256 | tf_op jit(solution)/shard_map/psum | solution.py:100
  72.8 11.4 %reduce-scatter.2.cloned.1.call-done = f32[32,2,6,32]{3,0,2,1:T(8,128)} async-done(((f32[128,2,6,32]{3,0,2,1:T(8,128)}), f32[32,2,6,32]{3,0,2,1:T(8,128)}) %reduce-scatter.2.cloned.1.call-update) | async-done | bytes 49168 | tf_op jit(solution)/shard_map/reduce_scatter | solution.py:108
  84.2 1.0 slice_bitcast_fusion
  86.1 1.0 fusion.29
  87.1 1.4 subtract_subtract_fusion
  88.4 1.0 fusion.186
  89.4 1.0 fusion.187
  90.4 1.0 fusion.188
  91.4 1.0 fusion.74
  92.3 1.8 %fusion.89 = f32[32,32,64]{2,1,0:T(8,128)S(1)} fusion(f32[32,32,64]{2,1,0:T(8,128)S(1)} %get-tuple-element.63, f32[32,32,64]{2,1,0:T(8,128)S(1)} %get-tuple-element.60, f32[32]{0:T(128)S(1)} %get-tuple-element.57, f32[32,32]{1,0:T(8,128)S(1)} %copy.51, f32[32,64]{1,0:T(8,128)S(1)} %copy-done.5), kind=kOutput, calls=%fused_computation.55 | output fusion | flops 394303 | bytes 798848 | tf_op jit(solution)/shard_map/div | solution.py:48
  94.2 1.8 %fusion.92 = f32[32,32,64]{2,1,0:T(8,128)S(1)} fusion(f32[32,32,64]{2,1,0:T(8,128)S(1)} %get-tuple-element.65, f32[32,32,64]{2,1,0:T(8,128)S(1)} %get-tuple-element.62, f32[32]{0:T(128)S(1)} %get-tuple-element.56, f32[32,32]{1,0:T(8,128)S(1)} %copy.53, f32[32,64]{1,0:T(8,128)S(1)} %copy-done.5), kind=kOutput, calls=%fused_computation.58 | output fusion | flops 394303 | bytes 798848 | tf_op jit(solution)/shard_map/div | solution.py:48
  96.0 1.8 %fusion.95 = f32[32,32,64]{2,1,0:T(8,128)S(1)} fusion(f32[32,32,64]{2,1,0:T(8,128)S(1)} %get-tuple-element.67, f32[32,32,64]{2,1,0:T(8,128)S(1)} %get-tuple-element.64, f32[32]{0:T(128)S(1)} %get-tuple-element.55, f32[32,32]{1,0:T(8,128)S(1)} %copy.55, f32[32,64]{1,0:T(8,128)S(1)} %copy-done.5), kind=kOutput, calls=%fused_computation.61 | output fusion | flops 394303 | bytes 798848 | tf_op jit(solution)/shard_map/div | solution.py:48
  97.9 1.8 %fusion.98 = f32[32,32,64]{2,1,0:T(8,128)S(1)} fusion(f32[32,32,64]{2,1,0:T(8,128)S(1)} %fusion.74, f32[32,32,64]{2,1,0:T(8,128)S(1)} %get-tuple-element.66, f32[32]{0:T(128)S(1)} %get-tuple-element.54, f32[32,32]{1,0:T(8,128)S(1)} %copy.57, f32[32,64]{1,0:T(8,128)S(1)} %copy-done.5), kind=kOutput, calls=%fused_computation.64 | output fusion | flops 394303 | bytes 798848 | tf_op jit(solution)/shard_map/div | solution.py:48
  99.7 2.0 %fusion.189 = f32[32,64]{1,0:T(8,128)S(1)} fusion(f32[32]{0:T(128)S(1)} %get-tuple-element.54, f32[32,32,64]{2,1,0:T(8,128)S(1)} %get-tuple-element.66, f32[32,32,64]{2,1,0:T(8,128)S(1)} %fusion.74, f32[32,32,64]{2,1,0:T(8,128)S(1)} %fusion.98, f32[32,32,64]{2,1,0:T(8,128)S(1)} %fusion.95, f32[32,32,64]{2,1,0:T(8,128)S(1)} %fusion.92, ...), kind=kOutput, calls=%fused_computation.238 | output fusion | flops 1440831 | bytes 2138624 | tf_op jit(solution)/shard_map/div | solution.py:48
  101.8 17.4 %psum.22 = f32[32,64]{1,0:T(8,128)S(1)} all-reduce(f32[32,64]{1,0:T(8,128)S(1)} %fusion.179), channel_id=1, replica_groups=mesh['groups'=2,'loans'=4,'paths'=4] {'loans'}, use_global_device_ids=true, to_apply=%region_13.14 | all-reduce | flops 2048 | bytes 16384 | tf_op jit(solution)/shard_map/psum | solution.py:129
  119.2 10.1 %psum.23 = f32[32,64]{1,0:T(8,128)S(1)} all-reduce(f32[32,64]{1,0:T(8,128)S(1)} %psum.22), channel_id=1, replica_groups=mesh['groups'=2,'loans'=4,'paths'=4] {'paths'}, use_global_device_ids=true, to_apply=%region_14.15 | all-reduce | flops 2048 | bytes 16384 | tf_op jit(solution)/shard_map/psum | solution.py:130
  (46 shorter events, 3.9 us)
Async XLA Ops:
  6.5 3.9 %copy-start = (bf16[1024,128]{1,0:T(8,128)(2,1)S(1)}, bf16[1024,128]{1,0:T(8,128)(2,1)}, u32[]{:S(2)}) copy-start(bf16[1024,128]{1,0:T(8,128)(2,1)} %param.14) | copy-start | bytes 786436
  6.5 41.8 %copy-start.1 = (f32[1024]{0:T(1024)S(1)}, f32[1024]{0:T(1024)}, u32[]{:S(2)}) copy-start(f32[1024]{0:T(1024)} %param.16) | copy-start | bytes 12292
  6.5 41.8 %copy-start.2 = (f32[1024]{0:T(1024)S(1)}, f32[1024]{0:T(1024)}, u32[]{:S(2)}) copy-start(f32[1024]{0:T(1024)} %param.17) | copy-start | bytes 12292
  6.5 37.1 %all-gather.2.cloned.1.call-start = ((), (), s32[]{:S(2)}) async-start(), calls=%async_computation.1 | async-start | bytes 1597440 | tf_op jit(solution)/shard_map/all_gather | solution.py:79
  7.3 77.0 %reduce-scatter.2.cloned.1.call-start = ((), (), s32[]{:S(2)}) async-start(), calls=%async_computation.2 | async-start | bytes 983040 | tf_op jit(solution)/shard_map/reduce_scatter | solution.py:108
  52.7 2.9 %copy-start.6 = (s32[1024]{0:T(1024)S(1)}, s32[1024]{0:T(1024)}, u32[]{:S(2)}) copy-start(s32[1024]{0:T(1024)} %param.21) | copy-start | bytes 12292
  55.7 6.2 %copy-start.3 = (f32[32,64]{1,0:T(8,128)S(1)}, f32[32,64]{1,0:T(8,128)}, u32[]{:S(2)}) copy-start(f32[32,64]{1,0:T(8,128)} %param.26) | copy-start | bytes 24580
  55.7 16.5 %copy-start.4 = (s32[32,64]{1,0:T(8,128)S(1)}, s32[32,64]{1,0:T(8,128)}, u32[]{:S(2)}) copy-start(s32[32,64]{1,0:T(8,128)} %param.25) | copy-start | bytes 24580
  55.7 16.9 %copy-start.5 = (f32[32,64]{1,0:T(8,128)S(1)}, f32[32,64]{1,0:T(8,128)}, u32[]{:S(2)}) copy-start(f32[32,64]{1,0:T(8,128)} %param.27) | copy-start | bytes 24580
Sparse Core Ops, SparseCore 0:
  8.9 34.6 all-gather.1
  61.9 22.3 reduce-scatter.1
where the time goes:
time: 137 us
  waiting for transfers between devices  42.8 us (31%)
  blocking collectives  37.6 us (27%)
  other arithmetic  21 us (15%)
  matrix products  18 us (13%)
  between operations  13.7 us (10%)
  local copies, waits for them, and re-layouts  3.61 us (3%)
    all_gather x1, waiting for transfers between devices, on_device(): piece = lax.all_gather(region_hpi, 'loans', axis=0, tiled=True)  30.7 us
    psum x1, blocking collectives, on_device(): mine = lax.psum(ordered, 'loans')  17.4 us
    reduce_scatter x1, waiting for transfers between devices, on_device(): lax.psum_scatter(jnp.dot(block, onehot_deal, precision=highest).reshape(p...  11.4 us
    psum x1, blocking collectives, on_device(): totals = lax.psum(jnp.dot(balance, onehot_deal, precision=highest), 'loans')  10.2 us
    psum x1, blocking collectives, on_device(): total = lax.psum(mine, 'paths')  10.1 us
    div x5, other arithmetic, waterfall(): flow = paid + inter[:, :, step, None] * coupon_due / denom  9.33 us
    dot_general x6, matrix products, waterfall(): jnp.einsum('xpj,xjk->xpk', held, ahead_mask, precision=lax.Precision.HIGH...  6.23 us
    unnamed x6, other arithmetic  6.19 us
  transfers between devices with their start and end apart: 2, of which 2 were waited for; matrix products, arithmetic and copies ran while one was open for 5% of the time, Pallas kernels for 0%

commit v1 on v0

--- a/solution.py
+++ b/solution.py
@@ -1,6 +1,10 @@
+import functools
+
 import jax
 import jax.numpy as jnp
 from jax import lax
+from jax.experimental import pallas as pl
+from jax.experimental.pallas import tpu as pltpu
 from jax.sharding import PartitionSpec as P
 
 prepay_base = -4.0
@@ -8,6 +12,7 @@
 default_base = -6.0
 price_sens = 12.0
 oas_spread = 0.005
+CHUNK = 512
 
 
 def loan_month(held, covar, coupon, rate_month, sched_rate, mortgage_now, hpi_now):
@@ -132,6 +137,307 @@
     return 100.0 * (total / all_paths - 1.0)
 
 
+MESH = pl.DeviceIdType.MESH
+
+
+def rows_of(x):
+    return x.reshape((1,) + x.shape)
+
+
+def pool_kernel(groups, lanes_out, chunk,
+                feat, coef, coupon, balance, term, age, region, deal, hpi, rates, owner, order, share, trate,
+                out,
+                loan_tx, loan_rx, hpi_tx, hpi_rx, left, marks, cash, pool, table, cols, part, part_rx, half, half_rx,
+                loan_ss, loan_rs, hpi_ss, hpi_rs, part_ss, part_rs, half_ss, half_rs, own_sem):
+    n_loans, n_paths = groups
+    f32, bf16 = jnp.float32, jnp.bfloat16
+    me = lax.axis_index("loans")
+    me_path = lax.axis_index("paths")
+    n = coupon.shape[1]
+    rows, steps, paths = hpi.shape
+    here = paths // n_loans
+    wide = hpi_tx.shape[2]
+    deals, tranches = share.shape
+    copies = lanes_out // deals
+
+    barrier = pltpu.get_barrier_semaphore()
+    for off in range(1, n_loans):
+        pl.semaphore_signal(barrier, inc=1, device_id={"loans": lax.rem(me + off, n_loans)}, device_id_type=MESH)
+    for off in range(1, n_paths):
+        pl.semaphore_signal(barrier, inc=1, device_id={"paths": lax.rem(me_path + off, n_paths)}, device_id_type=MESH)
+
+    covar = lax.dot_general(coef[...], feat[...], (((0,), (1,)), ((), ())), preferred_element_type=f32)
+    note = coupon[...]
+    place = region[...]
+    place = place + (place // rows) * (wide - rows)
+    loan_tx[...] = jnp.concatenate(
+        [
+            0.5 * (covar[0:1, :] + prepay_base + incentive * note),
+            0.5 * (covar[1:2, :] + default_base),
+            note / 12.0,
+            balance[...],
+            (term[...] - age[...]).astype(f32),
+            place.astype(f32),
+            deal[...].astype(f32),
+            jnp.zeros((1, n), f32),
+        ],
+        axis=0,
+    )
+    for step in range(steps):
+        block = hpi[:, step, :] * (-0.5 * price_sens)
+        if wide > rows:
+            block = jnp.concatenate([block, jnp.zeros((wide - rows, paths), f32)], axis=0)
+        hpi_tx[step] = block.T
+
+    pl.semaphore_wait(barrier, n_loans + n_paths - 2)
+    loan_copies, hpi_copies = [], []
+    for off in range(1, n_loans):
+        there = lax.rem(me + off, n_loans)
+        loan_copies.append(pltpu.make_async_remote_copy(
+            src_ref=loan_tx, dst_ref=loan_rx.at[me], send_sem=loan_ss.at[off], recv_sem=loan_rs.at[off],
+            device_id={"loans": there}, device_id_type=MESH))
+        hpi_copies.append(pltpu.make_async_remote_copy(
+            src_ref=hpi_tx.at[:, pl.ds(pl.multiple_of(there * here, here), here), :],
+            dst_ref=hpi_rx.at[me], send_sem=hpi_ss.at[off], recv_sem=hpi_rs.at[off],
+            device_id={"loans": there}, device_id_type=MESH))
+    for copy in loan_copies:
+        copy.start()
+    for copy in hpi_copies:
+        copy.start()
+    own_loan = pltpu.make_async_copy(loan_tx, loan_rx.at[me], own_sem.at[0])
+    own_hpi = pltpu.make_async_copy(
+        hpi_tx.at[:, pl.ds(pl.multiple_of(me * here, here), here), :], hpi_rx.at[me], own_sem.at[1])
+    own_loan.start()
+    own_hpi.start()
+
+    ids = lax.broadcasted_iota(jnp.int32, (deals, 128), 0)
+    key = (jnp.broadcast_to(owner[...], (deals, 128)) * deals + ids).astype(f32)
+    key_row = key.T[:deals, :]
+    below = jnp.where(key[:, :deals] < key_row, 1.0, 0.0).astype(f32)
+    spot = jnp.sum(below, axis=0, keepdims=True)
+    perm = jnp.where(spot == lax.broadcasted_iota(jnp.int32, (deals, deals), 0).astype(f32), 1.0, 0.0).astype(f32)
+    listing = jnp.sum(perm * lax.broadcasted_iota(jnp.int32, (deals, deals), 1).astype(f32), axis=1, keepdims=True)
+    listing = jnp.concatenate([listing] * copies, axis=0)
+
+    def spread(x):
+        x = jnp.dot(perm, x, preferred_element_type=f32, precision=lax.Precision.HIGHEST)
+        x = jnp.concatenate([x, jnp.zeros((deals, 128 - tranches), f32)], axis=1)
+        return jnp.concatenate([x] * copies, axis=0).T[:tranches, :]
+
+    table[...] = spread(order[...].astype(f32))
+    share_t = spread(share[...])
+    rate_t = spread(trate[...])
+    names = lax.broadcasted_iota(jnp.int32, (tranches, lanes_out), 0).astype(f32)
+
+    def walk(j, carry):
+        run, upto = carry
+        hit = names == table[pl.ds(j, 1), :]
+        run = run + jnp.sum(jnp.where(hit, share_t, 0.0), axis=0, keepdims=True)
+        return run, jnp.where(hit, run, upto)
+
+    whole, upto = lax.fori_loop(
+        0, tranches, walk, (jnp.zeros((1, lanes_out), f32), jnp.zeros((tranches, lanes_out), f32)), unroll=4)
+    weight = share_t / whole
+    upto = upto / whole
+    per_weight = 1.0 / weight
+    due_t = rate_t * weight
+
+    stack = jnp.concatenate([rates[0], rates[1], jnp.zeros((128 - 2 * steps, paths), f32)], axis=0)
+    cols[...] = stack.T
+    mine = cols[pl.ds(pl.multiple_of(me * here, here), here), :]
+    mort = [(0.5 * incentive) * mine[:, steps + t:steps + t + 1] for t in range(steps)]
+    disc = []
+    total = jnp.zeros((here, 1), f32)
+    for t in range(steps):
+        total = total + (mine[:, t:t + 1] + oas_spread)
+        disc.append(jnp.exp(-total / 12.0))
+
+    own_loan.wait()
+    for copy in loan_copies:
+        copy.wait_recv()
+    ages = lax.broadcasted_iota(jnp.int32, (8, n), 0).astype(f32)
+    for src in range(n_loans):
+        r = loan_rx[src, 2:3, :]
+        grown = 1.0 + r
+        log = jnp.log(grown) * (r / (grown - 1.0))
+        x = (loan_rx[src, 4:5, :] - ages) * log
+        left[src] = r / (jnp.exp(x) - 1.0)
+    pool[...] = jnp.zeros(pool.shape, f32)
+    own_hpi.wait()
+    for copy in hpi_copies:
+        copy.wait_recv()
+    height = steps * here
+    for src in range(n_loans):
+        x = hpi_rx[src].reshape(height, wide)
+        high = x.astype(bf16)
+        marks[0:height, src * wide:(src + 1) * wide] = high
+        marks[height:2 * height, src * wide:(src + 1) * wide] = (x - high.astype(f32)).astype(bf16)
+
+    depth = n_loans * wide
+    per = n // chunk
+
+    def work(c, _):
+        src = c // per
+        lane = pl.ds(pl.multiple_of((c % per) * chunk, chunk), chunk)
+        lv = loan_rx[src, :, lane]
+        sched_rate = left[src, :, lane]
+        pick = jnp.where(
+            lax.broadcasted_iota(jnp.int32, (depth, chunk), 0) == lv[5:6, :].astype(jnp.int32), 1.0, 0.0).astype(bf16)
+        got = jnp.dot(marks[...], pick, preferred_element_type=f32)
+        held = jnp.broadcast_to(lv[3:4, :], (here, chunk))
+        r = lv[2:3, :]
+        for t in range(steps):
+            h = got[t * here:(t + 1) * here] + got[height + t * here:height + (t + 1) * here]
+            smm = 0.5 + 0.5 * jnp.tanh(lv[0:1, :] - mort[t])
+            mdr = 0.5 + 0.5 * jnp.tanh(lv[1:2, :] + h)
+            interest = held * r
+            sched = held * sched_rate[t:t + 1, :]
+            lost = mdr * held
+            principal = sched + smm * (held - sched - lost) + lost
+            held = held - principal
+            base = t * 4 * here
+            for k, x in enumerate((principal, interest)):
+                high = x.astype(bf16)
+                cash[base + k * here:base + (k + 1) * here, :] = high
+                cash[base + (k + 2) * here:base + (k + 3) * here, :] = (x - high.astype(f32)).astype(bf16)
+        b = jnp.broadcast_to(lv[3:4, :], (16, chunk))
+        high = b.astype(bf16)
+        cash[4 * height:4 * height + 16, :] = high
+        cash[4 * height + 16:4 * height + 32, :] = (b - high.astype(f32)).astype(bf16)
+        member = jnp.where(listing == lv[6:7, :], 1.0, 0.0).astype(bf16)
+        pool[...] += lax.dot_general(cash[...], member, (((1,), (1,)), ((), ())), preferred_element_type=f32)
+        return 0
+
+    lax.fori_loop(0, n_loans * per, work, 0)
+
+    start = pool[4 * height:4 * height + 1, :] + pool[4 * height + 16:4 * height + 17, :]
+    per_start = 1.0 / start
+    sub = here // copies
+    group = lax.broadcasted_iota(jnp.int32, (sub, lanes_out), 1) // deals
+
+    def packed(x):
+        x = jnp.broadcast_to(x, (here, lanes_out))
+        y = x[0:sub]
+        for c in range(1, copies):
+            y = jnp.where(group == c, x[c * sub:(c + 1) * sub], y)
+        return y
+
+    paid_upto = jnp.zeros((sub, lanes_out), f32)
+    gone, gains, fall = [], [], []
+    for t in range(steps):
+        base = t * 4 * here
+        princ = packed(pool[base:base + here, :] + pool[base + 2 * here:base + 3 * here, :])
+        inter = packed(pool[base + here:base + 2 * here, :] + pool[base + 3 * here:base + 4 * here, :])
+        paid_upto = paid_upto + jnp.maximum(princ, 0.0)
+        gone.append(paid_upto * per_start)
+        gains.append(inter * per_start)
+        fall.append(packed(disc[t]))
+    worth = jnp.zeros((tranches, lanes_out), f32)
+    for j in range(sub):
+        frac = jnp.ones((tranches, lanes_out), f32)
+        for t in range(steps):
+            d = fall[t][j:j + 1, :]
+            later = jnp.clip((upto - gone[t][j:j + 1, :]) * per_weight, 0.0, 1.0)
+            denom = jnp.sum(due_t * frac, axis=0, keepdims=True)
+            flow = (frac - later) + (gains[t][j:j + 1, :] / denom) * (rate_t * frac)
+            worth = worth + flow * d
+            frac = later
+        worth = worth + frac * d
+    wt = jnp.concatenate([worth, jnp.zeros((128 - tranches, lanes_out), f32)], axis=0).T
+    acc = wt[0:deals]
+    for c in range(1, copies):
+        acc = acc + wt[c * deals:(c + 1) * deals]
+    part[...] = acc
+    part_copies = []
+    for off in range(1, n_loans):
+        part_copies.append(pltpu.make_async_remote_copy(
+            src_ref=part, dst_ref=part_rx.at[me], send_sem=part_ss.at[off], recv_sem=part_rs.at[off],
+            device_id={"loans": lax.rem(me + off, n_loans)}, device_id_type=MESH))
+    for copy in part_copies:
+        copy.start()
+    part_rx[me] = acc
+    for copy in part_copies:
+        copy.wait_recv()
+    acc = part_rx[0]
+    for src in range(1, n_loans):
+        acc = acc + part_rx[src]
+    half[...] = acc
+    half_copies = []
+    for off in range(1, n_paths):
+        half_copies.append(pltpu.make_async_remote_copy(
+            src_ref=half, dst_ref=half_rx.at[me_path], send_sem=half_ss.at[off], recv_sem=half_rs.at[off],
+            device_id={"paths": lax.rem(me_path + off, n_paths)}, device_id_type=MESH))
+    for copy in half_copies:
+        copy.start()
+    half_rx[me_path] = acc
+    for copy in half_copies:
+        copy.wait_recv()
+    acc = half_rx[0]
+    for src in range(1, n_paths):
+        acc = acc + half_rx[src]
+    out[...] = (100.0 * (acc / (paths * n_paths) - 1.0))[:, :tranches]
+    for copy in loan_copies + hpi_copies + part_copies + half_copies:
+        copy.wait_send()
+
+
+def fused(loan_features, hazard_coef, coupon, balance, loan_term, loan_age, loan_region, loan_deal,
+          region_hpi, rate_paths, deal_owner, tranche_order, tranche_share, tranche_rate):
+    n_loans, n_paths = lax.axis_size("loans"), lax.axis_size("paths")
+    n = coupon.shape[0]
+    rows, steps, paths = region_hpi.shape
+    deals, tranches = tranche_share.shape
+    here = paths // n_loans
+    wide = -(-rows // 128) * 128
+    lanes_out = 128
+    chunk = min(n, CHUNK)
+    height = steps * here
+    f32 = jnp.float32
+    dma = pltpu.SemaphoreType.DMA
+    return pl.pallas_call(
+        functools.partial(pool_kernel, (n_loans, n_paths), lanes_out, chunk),
+        out_shape=jax.ShapeDtypeStruct((deals, tranches), f32),
+        in_specs=[pl.BlockSpec(memory_space=pltpu.VMEM)] * 14,
+        out_specs=pl.BlockSpec(memory_space=pltpu.VMEM),
+        scratch_shapes=[
+            pltpu.VMEM((8, n), f32),
+            pltpu.VMEM((n_loans, 8, n), f32),
+            pltpu.VMEM((steps, paths, wide), f32),
+            pltpu.VMEM((n_loans, steps, here, wide), f32),
+            pltpu.VMEM((n_loans, 8, n), f32),
+            pltpu.VMEM((2 * height, n_loans * wide), jnp.bfloat16),
+            pltpu.VMEM((4 * height + 32, chunk), jnp.bfloat16),
+            pltpu.VMEM((4 * height + 32, lanes_out), f32),
+            pltpu.VMEM((tranches, lanes_out), f32),
+            pltpu.VMEM((paths, 128), f32),
+            pltpu.VMEM((deals, 128), f32),
+            pltpu.VMEM((n_loans, deals, 128), f32),
+            pltpu.VMEM((deals, 128), f32),
+            pltpu.VMEM((n_paths, deals, 128), f32),
+            dma((n_loans,)), dma((n_loans,)), dma((n_loans,)), dma((n_loans,)),
+            dma((n_loans,)), dma((n_loans,)), dma((n_paths,)), dma((n_paths,)), dma((2,)),
+        ],
+        compiler_params=pltpu.CompilerParams(collective_id=0, has_side_effects=True),
+    )(loan_features, hazard_coef, rows_of(coupon), rows_of(balance), rows_of(loan_term), rows_of(loan_age),
+      rows_of(loan_region), rows_of(loan_deal), region_hpi, rate_paths, deal_owner, tranche_order,
+      tranche_share, tranche_rate)
+
+
+def fits(args):
+    n = args[2].shape[0]
+    paths = args[8].shape[2]
+    deals, tranches = args[12].shape
+    n_loans = lax.axis_size("loans")
+    return (
+        paths == 128 and deals % 8 == 0 and 128 % deals == 0 and tranches <= 128 and tranches % 8 == 0
+        and paths % (32 * n_loans) == 0 and (paths // n_loans) % (8 * (128 // deals)) == 0
+        and n % min(n, CHUNK) == 0 and n % 128 == 0 and args[8].shape[0] % 8 == 0 and args[9].shape[1] <= 8
+    )
+
+
+def device_program(*args):
+    return fused(*args) if fits(args) else on_device(*args)
+
+
 def solution(mesh):
     in_specs = (
         P(("groups", "loans"), None),
@@ -151,5 +457,5 @@
     )
     out_specs = P("groups", None)
     return jax.shard_map(
-        on_device, mesh=mesh, in_specs=in_specs, out_specs=out_specs, check_vma=False
-    )
+        device_program, mesh=mesh, in_specs=in_specs, out_specs=out_specs, check_vma=False
+    )

time: 137 us -> 40.5 us (0.30)
  waiting for transfers between devices: 42.8 us -> 0 us
  blocking collectives: 37.6 us -> 0 us
  Pallas kernels: 0 us -> 34.2 us
  other arithmetic: 21 us -> 0 us
  matrix products: 18 us -> 0 us
  between operations: 13.7 us -> 0.01 us
  local copies, waits for them, and re-layouts: 3.61 us -> 5.9 us
    psum x3 -> x0, blocking collectives: 37.6 us -> none  [the longest x1 17.4 us: on_device(): mine = lax.psum(ordered, 'loans')]
    pallas_call x0 -> x1, Pallas kernels: none -> 34.2 us  [fused(): pl.pallas_call(functools.partial(pool_kernel, (n_loans, n_paths), lanes_o...]
    all_gather x1 -> x0, waiting for transfers between devices: 30.7 us -> none  [on_device(): piece = lax.all_gather(region_hpi, 'loans', axis=0, tiled=True)]
    dot_general x11 -> x0, matrix products: 18 us -> none  [the longest x6 6.23 us: waterfall(): jnp.einsum('xpj,xjk->xpk', held, ahead_mask, precision=lax.Precision.HIGH...]
    reduce_scatter x1 -> x0, waiting for transfers between devices: 11.4 us -> none  [on_device(): lax.psum_scatter(jnp.dot(block, onehot_deal, precision=highest).reshape(p...]
    div x7 -> x0, other arithmetic: 10.8 us -> none  [the longest x5 9.33 us: waterfall(): flow = paid + inter[:, :, step, None] * coupon_due / denom]
    unnamed x6 -> x0, other arithmetic: 6.19 us -> none
    unnamed x15 -> x11, local copies, waits for them, and re-layouts: 0.24 us -> 5.9 us
  transfers between devices with their start and end apart: 2 -> 0, of which waited for: 2 -> 0; matrix products, arithmetic and copies ran while one was open for 5% -> 0% of each run, Pallas kernels for 0% -> 0%
where the time goes in v1:
time: 40.5 us; the launch traced here: 40.2 us
  Pallas kernels  34.2 us (84%)
  local copies, waits for them, and re-layouts  5.9 us (15%)
    pallas_call x1, Pallas kernels, fused(): pl.pallas_call(functools.partial(pool_kernel, (n_loans, n_paths), lanes_o...  34.2 us
    unnamed x11, local copies, waits for them, and re-layouts  5.9 us

profile of v1, /device:TPU:0, one launch (start us, length us, event | category | flops | bytes accessed | tf_op | source)
XLA Modules:
  0.0 40.2 jit_solution(15421862393486086934)
XLA Ops:
  0.0 0.0 copy-start
  0.0 0.7 %copy-done = f32[2,6,128]{2,0,1:T(2,128)S(1)} copy-done((f32[2,6,128]{2,0,1:T(2,128)S(1)}, f32[2,6,128]{2,0,1:T(2,128)}, u32[]{:S(2)}) %copy-start) | copy-done | bytes 6168
  0.7 0.0 copy-start.2
  0.7 0.6 %copy.17.rates = f32[2,6,128]{2,1,0:T(8,128)} copy(f32[2,6,128]{2,0,1:T(2,128)S(1)} %copy-done) | data formatting | bytes 12288 | tf_op args[9]
  1.3 0.1 copy-done.2
  1.4 0.0 copy-start.1
  1.4 0.7 %copy.18.owner = s32[32,1]{1,0:T(8,128)} copy(s32[32,1]{0,1:T(1,128)S(1)} %copy-done.2) | data formatting | bytes 256 | tf_op args[10]
  2.0 0.0 copy-done.1
  2.0 0.7 %copy.15.coef = bf16[128,2]{1,0:T(8,128)(2,1)} copy(bf16[128,2]{0,1:T(2,128)(2,1)S(1)} %copy-done.1) | data formatting | bytes 1024 | tf_op args[1]
  2.8 1.8 %copy.16.hpi = f32[104,6,128]{2,1,0:T(8,128)} copy(f32[104,6,128]{2,0,1:T(8,128)} %param.22) | data formatting | bytes 638976 | tf_op args[8]
  4.6 34.2 %shard_map.136 = f32[32,64]{1,0:T(8,128)} custom-call(bf16[1024,128]{1,0:T(8,128)(2,1)} %feat.1, bf16[128,2]{1,0:T(8,128)(2,1)} %copy.15.coef, f32[1,1024]{1,0:T(1,128)} %bitcast.6, f32[1,1024]{1,0:T(1,128)} %bitcast.7, s32[1,1024]{1,0:T(1,128)} %bitcast.8, s32[1,1024]{1,0:T(1,128)} %bitcast.9, s32[1,1024]{1,0:T(1,128)} %bitcast.10, s32[1,1024]{1,0:T(1,128)} %bitcast.11, ...), custom_call_target="tpu_custom_call" | custom-call | tf_op jit(solution)/shard_map/pallas_call | solution.py:396
  38.8 1.3 %copy.20 = f32[32,64]{1,0:T(8,128)} copy(f32[32,64]{1,0:T(8,128)} %shard_map.136) | data formatting | bytes 16384
Async XLA Ops:
  0.0 0.7 %copy-start = (f32[2,6,128]{2,0,1:T(2,128)S(1)}, f32[2,6,128]{2,0,1:T(2,128)}, u32[]{:S(2)}) copy-start(f32[2,6,128]{2,0,1:T(2,128)} %param.23) | copy-start | bytes 18436
  0.7 0.7 %copy-start.2 = (s32[32,1]{0,1:T(1,128)S(1)}, s32[32,1]{0,1:T(1,128)}, u32[]{:S(2)}) copy-start(s32[32,1]{0,1:T(1,128)} %param.24) | copy-start | bytes 388
  1.4 0.7 %copy-start.1 = (bf16[128,2]{0,1:T(2,128)(2,1)S(1)}, bf16[128,2]{0,1:T(2,128)(2,1)}, u32[]{:S(2)}) copy-start(bf16[128,2]{0,1:T(2,128)(2,1)} %param.15) | copy-start | bytes 1540

commit v2 on v1

--- a/solution.py
+++ b/solution.py
@@ -12,7 +12,7 @@
 default_base = -6.0
 price_sens = 12.0
 oas_spread = 0.005
-CHUNK = 512
+EARLY = 4
 
 
 def loan_month(held, covar, coupon, rate_month, sched_rate, mortgage_now, hpi_now):
@@ -144,19 +144,21 @@
     return x.reshape((1,) + x.shape)
 
 
-def pool_kernel(groups, lanes_out, chunk,
+def pool_kernel(groups, lanes_out,
                 feat, coef, coupon, balance, term, age, region, deal, hpi, rates, owner, order, share, trate,
                 out,
-                loan_tx, loan_rx, hpi_tx, hpi_rx, left, marks, cash, pool, table, cols, part, part_rx, half, half_rx,
-                loan_ss, loan_rs, hpi_ss, hpi_rs, part_ss, part_rs, half_ss, half_rs, own_sem):
+                loan_tx, loan_rx, hpi_tx, hpi_rx, end_tx, end_rx, left, marks, end_marks, picks, balances, cash, pool, table, cols,
+                part, part_rx, half, half_rx,
+                loan_ss, loan_rs, hpi_ss, hpi_rs, end_ss, end_rs, part_ss, part_rs, half_ss, half_rs, own_sem):
     n_loans, n_paths = groups
     f32, bf16 = jnp.float32, jnp.bfloat16
     me = lax.axis_index("loans")
     me_path = lax.axis_index("paths")
     n = coupon.shape[1]
-    rows, steps, paths = hpi.shape
+    steps, rows, paths = hpi.shape
     here = paths // n_loans
-    wide = hpi_tx.shape[2]
+    wide = -(-rows // 128) * 128
+    split = end_tx.shape[1]
     deals, tranches = share.shape
     copies = lanes_out // deals
 
@@ -166,7 +168,7 @@
     for off in range(1, n_paths):
         pl.semaphore_signal(barrier, inc=1, device_id={"paths": lax.rem(me_path + off, n_paths)}, device_id_type=MESH)
 
-    covar = lax.dot_general(coef[...], feat[...], (((0,), (1,)), ((), ())), preferred_element_type=f32)
+    covar = lax.dot_general(coef[...], feat[...], (((1,), (1,)), ((), ())), preferred_element_type=f32)
     note = coupon[...]
     place = region[...]
     place = place + (place // rows) * (wide - rows)
@@ -183,37 +185,53 @@
         ],
         axis=0,
     )
-    for step in range(steps):
-        block = hpi[:, step, :] * (-0.5 * price_sens)
-        if wide > rows:
-            block = jnp.concatenate([block, jnp.zeros((wide - rows, paths), f32)], axis=0)
-        hpi_tx[step] = block.T
-
     pl.semaphore_wait(barrier, n_loans + n_paths - 2)
-    loan_copies, hpi_copies = [], []
+    loan_copies, hpi_copies, end_copies = [], [], []
     for off in range(1, n_loans):
         there = lax.rem(me + off, n_loans)
         loan_copies.append(pltpu.make_async_remote_copy(
             src_ref=loan_tx, dst_ref=loan_rx.at[me], send_sem=loan_ss.at[off], recv_sem=loan_rs.at[off],
             device_id={"loans": there}, device_id_type=MESH))
         hpi_copies.append(pltpu.make_async_remote_copy(
-            src_ref=hpi_tx.at[:, pl.ds(pl.multiple_of(there * here, here), here), :],
-            dst_ref=hpi_rx.at[me], send_sem=hpi_ss.at[off], recv_sem=hpi_rs.at[off],
+            src_ref=hpi_tx.at[there], dst_ref=hpi_rx.at[me], send_sem=hpi_ss.at[off], recv_sem=hpi_rs.at[off],
+            device_id={"loans": there}, device_id_type=MESH))
+        end_copies.append(pltpu.make_async_remote_copy(
+            src_ref=end_tx.at[there], dst_ref=end_rx.at[me], send_sem=end_ss.at[off], recv_sem=end_rs.at[off],
             device_id={"loans": there}, device_id_type=MESH))
     for copy in loan_copies:
         copy.start()
+    own_loan = pltpu.make_async_copy(loan_tx, loan_rx.at[me], own_sem.at[0])
+    own_loan.start()
+    blocks = [hpi[step] * (-0.5 * price_sens) for step in range(steps)]
+    quarter = lax.broadcasted_iota(jnp.int32, (rows, paths), 1) // here
+    for q in range(n_loans):
+        packs = None
+        for t in range(EARLY):
+            x = blocks[t] if t == q else pltpu.roll(blocks[t], ((t - q) % n_loans) * here, 1)
+            packs = x if packs is None else jnp.where(quarter == t, x, packs)
+        hpi_tx[q] = packs
     for copy in hpi_copies:
         copy.start()
-    own_loan = pltpu.make_async_copy(loan_tx, loan_rx.at[me], own_sem.at[0])
-    own_hpi = pltpu.make_async_copy(
-        hpi_tx.at[:, pl.ds(pl.multiple_of(me * here, here), here), :], hpi_rx.at[me], own_sem.at[1])
-    own_loan.start()
+    own_hpi = pltpu.make_async_copy(hpi_tx.at[me], hpi_rx.at[me], own_sem.at[1])
     own_hpi.start()
-
-    ids = lax.broadcasted_iota(jnp.int32, (deals, 128), 0)
-    key = (jnp.broadcast_to(owner[...], (deals, 128)) * deals + ids).astype(f32)
-    key_row = key.T[:deals, :]
-    below = jnp.where(key[:, :deals] < key_row, 1.0, 0.0).astype(f32)
+    pad = jnp.zeros((2 * split - rows, paths), f32)
+    for q in range(n_loans):
+        packs = None
+        for t in range(n_loans):
+            x = blocks[EARLY + t % 2]
+            x = x[:split] if t < 2 else jnp.concatenate([x[split:], pad], axis=0)
+            x = x if t == q else pltpu.roll(x, ((t - q) % n_loans) * here, 1)
+            packs = x if packs is None else jnp.where(quarter[:split] == t, x, packs)
+        end_tx[q] = packs
+    for copy in end_copies:
+        copy.start()
+    own_end = pltpu.make_async_copy(end_tx.at[me], end_rx.at[me], own_sem.at[2])
+    own_end.start()
+
+    key = (jnp.broadcast_to(owner[...], (deals, deals)) * deals
+           + lax.broadcasted_iota(jnp.int32, (deals, deals), 1)).astype(f32)
+    key_col = jnp.concatenate([key, jnp.zeros((128 - deals, deals), f32)], axis=0).T[:, :deals]
+    below = jnp.where(key_col < key, 1.0, 0.0).astype(f32)
     spot = jnp.sum(below, axis=0, keepdims=True)
     perm = jnp.where(spot == lax.broadcasted_iota(jnp.int32, (deals, deals), 0).astype(f32), 1.0, 0.0).astype(f32)
     listing = jnp.sum(perm * lax.broadcasted_iota(jnp.int32, (deals, deals), 1).astype(f32), axis=1, keepdims=True)
@@ -242,14 +260,14 @@
     per_weight = 1.0 / weight
     due_t = rate_t * weight
 
-    stack = jnp.concatenate([rates[0], rates[1], jnp.zeros((128 - 2 * steps, paths), f32)], axis=0)
+    stack = jnp.concatenate([rates[t] for t in range(steps)] + [jnp.zeros((128 - 2 * steps, paths), f32)], axis=0)
     cols[...] = stack.T
     mine = cols[pl.ds(pl.multiple_of(me * here, here), here), :]
-    mort = [(0.5 * incentive) * mine[:, steps + t:steps + t + 1] for t in range(steps)]
+    mort = [(0.5 * incentive) * mine[:, 2 * t + 1:2 * t + 2] for t in range(steps)]
     disc = []
     total = jnp.zeros((here, 1), f32)
     for t in range(steps):
-        total = total + (mine[:, t:t + 1] + oas_spread)
+        total = total + (mine[:, 2 * t:2 * t + 1] + oas_spread)
         disc.append(jnp.exp(-total / 12.0))
 
     own_loan.wait()
@@ -266,28 +284,24 @@
     own_hpi.wait()
     for copy in hpi_copies:
         copy.wait_recv()
-    height = steps * here
+    height = EARLY * here
+    tail = (steps - EARLY) * here
     for src in range(n_loans):
-        x = hpi_rx[src].reshape(height, wide)
+        x = hpi_rx[src]
+        if wide > rows:
+            x = jnp.concatenate([x, jnp.zeros((wide - rows, paths), f32)], axis=0)
+        x = x.T
         high = x.astype(bf16)
         marks[0:height, src * wide:(src + 1) * wide] = high
         marks[height:2 * height, src * wide:(src + 1) * wide] = (x - high.astype(f32)).astype(bf16)
 
     depth = n_loans * wide
-    per = n // chunk
-
-    def work(c, _):
-        src = c // per
-        lane = pl.ds(pl.multiple_of((c % per) * chunk, chunk), chunk)
-        lv = loan_rx[src, :, lane]
-        sched_rate = left[src, :, lane]
-        pick = jnp.where(
-            lax.broadcasted_iota(jnp.int32, (depth, chunk), 0) == lv[5:6, :].astype(jnp.int32), 1.0, 0.0).astype(bf16)
-        got = jnp.dot(marks[...], pick, preferred_element_type=f32)
-        held = jnp.broadcast_to(lv[3:4, :], (here, chunk))
+
+    def months(got, held, lv, sched_rate, first, last, size):
         r = lv[2:3, :]
-        for t in range(steps):
-            h = got[t * here:(t + 1) * here] + got[height + t * here:height + (t + 1) * here]
+        for t in range(first, last):
+            k = t - first
+            h = got[k * here:(k + 1) * here] + got[size + k * here:size + (k + 1) * here]
             smm = 0.5 + 0.5 * jnp.tanh(lv[0:1, :] - mort[t])
             mdr = 0.5 + 0.5 * jnp.tanh(lv[1:2, :] + h)
             interest = held * r
@@ -295,20 +309,53 @@
             lost = mdr * held
             principal = sched + smm * (held - sched - lost) + lost
             held = held - principal
-            base = t * 4 * here
+            base = k * 4 * here
             for k, x in enumerate((principal, interest)):
                 high = x.astype(bf16)
                 cash[base + k * here:base + (k + 1) * here, :] = high
                 cash[base + (k + 2) * here:base + (k + 3) * here, :] = (x - high.astype(f32)).astype(bf16)
-        b = jnp.broadcast_to(lv[3:4, :], (16, chunk))
+        return held
+
+    def early(src, _):
+        lv = loan_rx[src]
+        pick = jnp.where(
+            lax.broadcasted_iota(jnp.int32, (depth, n), 0) == lv[5:6, :].astype(jnp.int32), 1.0, 0.0).astype(bf16)
+        picks[src] = pick
+        got = jnp.dot(marks[...], pick, preferred_element_type=f32)
+        held = months(got, jnp.broadcast_to(lv[3:4, :], (here, n)), lv, left[src], 0, EARLY, height)
+        balances[src] = held
+        b = jnp.broadcast_to(lv[3:4, :], (16, n))
         high = b.astype(bf16)
         cash[4 * height:4 * height + 16, :] = high
         cash[4 * height + 16:4 * height + 32, :] = (b - high.astype(f32)).astype(bf16)
         member = jnp.where(listing == lv[6:7, :], 1.0, 0.0).astype(bf16)
-        pool[...] += lax.dot_general(cash[...], member, (((1,), (1,)), ((), ())), preferred_element_type=f32)
+        pool[0:4 * height + 32, :] += lax.dot_general(
+            cash[...], member, (((1,), (1,)), ((), ())), preferred_element_type=f32)
         return 0
 
-    lax.fori_loop(0, n_loans * per, work, 0)
+    lax.fori_loop(0, n_loans, early, 0)
+
+    own_end.wait()
+    for copy in end_copies:
+        copy.wait_recv()
+    for src in range(n_loans):
+        x = jnp.concatenate([end_rx[src], jnp.zeros((128 - split, paths), f32)], axis=0).T
+        upper = pltpu.roll(x[tail:], split, 1)
+        x = jnp.where(lax.broadcasted_iota(jnp.int32, (tail, wide), 1) < split, x[:tail], upper)
+        high = x.astype(bf16)
+        end_marks[0:tail, src * wide:(src + 1) * wide] = high
+        end_marks[tail:2 * tail, src * wide:(src + 1) * wide] = (x - high.astype(f32)).astype(bf16)
+
+    def late(src, _):
+        lv = loan_rx[src]
+        got = jnp.dot(end_marks[...], picks[src], preferred_element_type=f32)
+        months(got, balances[src], lv, left[src], EARLY, steps, tail)
+        member = jnp.where(listing == lv[6:7, :], 1.0, 0.0).astype(bf16)
+        pool[4 * height + 32:, :] += lax.dot_general(
+            cash[0:4 * tail, :], member, (((1,), (1,)), ((), ())), preferred_element_type=f32)
+        return 0
+
+    lax.fori_loop(0, n_loans, late, 0)
 
     start = pool[4 * height:4 * height + 1, :] + pool[4 * height + 16:4 * height + 17, :]
     per_start = 1.0 / start
@@ -325,7 +372,7 @@
     paid_upto = jnp.zeros((sub, lanes_out), f32)
     gone, gains, fall = [], [], []
     for t in range(steps):
-        base = t * 4 * here
+        base = t * 4 * here + (32 if t >= EARLY else 0)
         princ = packed(pool[base:base + here, :] + pool[base + 2 * here:base + 3 * here, :])
         inter = packed(pool[base + here:base + 2 * here, :] + pool[base + 3 * here:base + 4 * here, :])
         paid_upto = paid_upto + jnp.maximum(princ, 0.0)
@@ -345,8 +392,10 @@
         worth = worth + frac * d
     wt = jnp.concatenate([worth, jnp.zeros((128 - tranches, lanes_out), f32)], axis=0).T
     acc = wt[0:deals]
+    low = lax.broadcasted_iota(jnp.int32, (deals // 2, 128), 1) < 64
     for c in range(1, copies):
         acc = acc + wt[c * deals:(c + 1) * deals]
+    acc = jnp.where(low, acc[:deals // 2], pltpu.roll(acc[deals // 2:], 64, 1))
     part[...] = acc
     part_copies = []
     for off in range(1, n_loans):
@@ -375,8 +424,10 @@
     acc = half_rx[0]
     for src in range(1, n_paths):
         acc = acc + half_rx[src]
-    out[...] = (100.0 * (acc / (paths * n_paths) - 1.0))[:, :tranches]
-    for copy in loan_copies + hpi_copies + part_copies + half_copies:
+    acc = 100.0 * (acc / (paths * n_paths) - 1.0)
+    out[:deals // 2, :] = acc[:, :tranches]
+    out[deals // 2:, :] = pltpu.roll(acc, 64, 1)[:, :tranches]
+    for copy in loan_copies + hpi_copies + end_copies + part_copies + half_copies:
         copy.wait_send()
 
 
@@ -389,37 +440,43 @@
     here = paths // n_loans
     wide = -(-rows // 128) * 128
     lanes_out = 128
-    chunk = min(n, CHUNK)
+    split = -(-rows // 16) * 8
     height = steps * here
     f32 = jnp.float32
     dma = pltpu.SemaphoreType.DMA
     return pl.pallas_call(
-        functools.partial(pool_kernel, (n_loans, n_paths), lanes_out, chunk),
+        functools.partial(pool_kernel, (n_loans, n_paths), lanes_out),
         out_shape=jax.ShapeDtypeStruct((deals, tranches), f32),
         in_specs=[pl.BlockSpec(memory_space=pltpu.VMEM)] * 14,
         out_specs=pl.BlockSpec(memory_space=pltpu.VMEM),
         scratch_shapes=[
             pltpu.VMEM((8, n), f32),
             pltpu.VMEM((n_loans, 8, n), f32),
-            pltpu.VMEM((steps, paths, wide), f32),
-            pltpu.VMEM((n_loans, steps, here, wide), f32),
+            pltpu.VMEM((n_loans, rows, paths), f32),
+            pltpu.VMEM((n_loans, rows, paths), f32),
+            pltpu.VMEM((n_loans, split, paths), f32),
+            pltpu.VMEM((n_loans, split, paths), f32),
             pltpu.VMEM((n_loans, 8, n), f32),
-            pltpu.VMEM((2 * height, n_loans * wide), jnp.bfloat16),
-            pltpu.VMEM((4 * height + 32, chunk), jnp.bfloat16),
+            pltpu.VMEM((2 * EARLY * here, n_loans * wide), jnp.bfloat16),
+            pltpu.VMEM((2 * (steps - EARLY) * here, n_loans * wide), jnp.bfloat16),
+            pltpu.VMEM((n_loans, n_loans * wide, n), jnp.bfloat16),
+            pltpu.VMEM((n_loans, here, n), f32),
+            pltpu.VMEM((4 * EARLY * here + 32, n), jnp.bfloat16),
             pltpu.VMEM((4 * height + 32, lanes_out), f32),
             pltpu.VMEM((tranches, lanes_out), f32),
             pltpu.VMEM((paths, 128), f32),
-            pltpu.VMEM((deals, 128), f32),
-            pltpu.VMEM((n_loans, deals, 128), f32),
-            pltpu.VMEM((deals, 128), f32),
-            pltpu.VMEM((n_paths, deals, 128), f32),
+            pltpu.VMEM((deals // 2, 128), f32),
+            pltpu.VMEM((n_loans, deals // 2, 128), f32),
+            pltpu.VMEM((deals // 2, 128), f32),
+            pltpu.VMEM((n_paths, deals // 2, 128), f32),
             dma((n_loans,)), dma((n_loans,)), dma((n_loans,)), dma((n_loans,)),
-            dma((n_loans,)), dma((n_loans,)), dma((n_paths,)), dma((n_paths,)), dma((2,)),
+            dma((n_loans,)), dma((n_loans,)), dma((n_loans,)), dma((n_loans,)),
+            dma((n_paths,)), dma((n_paths,)), dma((3,)),
         ],
         compiler_params=pltpu.CompilerParams(collective_id=0, has_side_effects=True),
-    )(loan_features, hazard_coef, rows_of(coupon), rows_of(balance), rows_of(loan_term), rows_of(loan_age),
-      rows_of(loan_region), rows_of(loan_deal), region_hpi, rate_paths, deal_owner, tranche_order,
-      tranche_share, tranche_rate)
+    )(loan_features, hazard_coef.T, rows_of(coupon), rows_of(balance), rows_of(loan_term), rows_of(loan_age),
+      rows_of(loan_region), rows_of(loan_deal), region_hpi.transpose(1, 0, 2),
+      rate_paths.transpose(1, 0, 2), deal_owner.reshape(1, deals), tranche_order, tranche_share, tranche_rate)
 
 
 def fits(args):
@@ -427,10 +484,11 @@
     paths = args[8].shape[2]
     deals, tranches = args[12].shape
     n_loans = lax.axis_size("loans")
+    rows, steps = args[8].shape[:2]
     return (
-        paths == 128 and deals % 8 == 0 and 128 % deals == 0 and tranches <= 128 and tranches % 8 == 0
-        and paths % (32 * n_loans) == 0 and (paths // n_loans) % (8 * (128 // deals)) == 0
-        and n % min(n, CHUNK) == 0 and n % 128 == 0 and args[8].shape[0] % 8 == 0 and args[9].shape[1] <= 8
+        paths == 128 and n_loans == EARLY and steps == EARLY + 2 and rows % 8 == 0 and 64 < rows <= 128
+        and deals % 16 == 0 and 128 % deals == 0 and tranches == 64
+        and (paths // n_loans) % (8 * (128 // deals)) == 0 and n % 128 == 0 and n <= 2048
     )
 
 

time: 40.5 us -> 34.4 us (0.85)
  local copies, waits for them, and re-layouts: 5.9 us -> 1.32 us
  Pallas kernels: 34.2 us -> 32.8 us
    unnamed x11 -> x1, local copies, waits for them, and re-layouts: 5.9 us -> 1.32 us
    pallas_call x1, Pallas kernels: 34.2 us -> 32.8 us  [fused(): pl.pallas_call(functools.partial(pool_kernel, (n_loans, n_paths), lanes_o...]
where the time goes in v2:
time: 34.4 us; the launch traced here: 34.2 us
  Pallas kernels  32.8 us (95%)
  local copies, waits for them, and re-layouts  1.32 us (4%)
    pallas_call x1, Pallas kernels, fused(): pl.pallas_call(functools.partial(pool_kernel, (n_loans, n_paths), lanes_o...  32.8 us
    unnamed x1, local copies, waits for them, and re-layouts  1.32 us

profile of v2, /device:TPU:0, one launch (start us, length us, event | category | flops | bytes accessed | tf_op | source)
XLA Modules:
  0.0 34.2 jit_solution(15230327764073544323)
XLA Ops:
  0.0 32.8 %shard_map.136 = f32[32,64]{1,0:T(8,128)} custom-call(bf16[1024,128]{1,0:T(8,128)(2,1)} %feat.1, bf16[2,128]{1,0:T(2,128)(2,1)} %bitcast.18, f32[1,1024]{1,0:T(1,128)} %bitcast.12, f32[1,1024]{1,0:T(1,128)} %bitcast.13, s32[1,1024]{1,0:T(1,128)} %bitcast.14, s32[1,1024]{1,0:T(1,128)} %bitcast.15, s32[1,1024]{1,0:T(1,128)} %bitcast.16, s32[1,1024]{1,0:T(1,128)} %bitcast.17, ...), custom_call_target="tpu_custom_call" | custom-call | tf_op jit(solution)/shard_map/pallas_call | solution.py:447
  32.9 1.3 %copy.16 = f32[32,64]{1,0:T(8,128)} copy(f32[32,64]{1,0:T(8,128)} %shard_map.136) | data formatting | bytes 16384

commit v3 on v2

--- a/solution.py
+++ b/solution.py
@@ -12,7 +12,7 @@
 default_base = -6.0
 price_sens = 12.0
 oas_spread = 0.005
-EARLY = 4
+SPAN = 2
 
 
 def loan_month(held, covar, coupon, rate_month, sched_rate, mortgage_now, hpi_now):
@@ -147,9 +147,9 @@
 def pool_kernel(groups, lanes_out,
                 feat, coef, coupon, balance, term, age, region, deal, hpi, rates, owner, order, share, trate,
                 out,
-                loan_tx, loan_rx, hpi_tx, hpi_rx, end_tx, end_rx, left, marks, end_marks, picks, balances, cash, pool, table, cols,
+                loan_tx, loan_rx, hpi_tx, hpi_rx, left, marks, picks, members, balances, cash, pool, table, cols,
                 part, part_rx, half, half_rx,
-                loan_ss, loan_rs, hpi_ss, hpi_rs, end_ss, end_rs, part_ss, part_rs, half_ss, half_rs, own_sem):
+                loan_ss, loan_rs, pass_ss, pass_rs, hpi_ss, hpi_rs, part_ss, part_rs, half_ss, half_rs, own_sem):
     n_loans, n_paths = groups
     f32, bf16 = jnp.float32, jnp.bfloat16
     me = lax.axis_index("loans")
@@ -158,7 +158,8 @@
     steps, rows, paths = hpi.shape
     here = paths // n_loans
     wide = -(-rows // 128) * 128
-    split = end_tx.shape[1]
+    split = hpi_tx.shape[2]
+    spans = steps // SPAN
     deals, tranches = share.shape
     copies = lanes_out // deals
 
@@ -172,7 +173,7 @@
     note = coupon[...]
     place = region[...]
     place = place + (place // rows) * (wide - rows)
-    loan_tx[...] = jnp.concatenate(
+    bundle = jnp.concatenate(
         [
             0.5 * (covar[0:1, :] + prepay_base + incentive * note),
             0.5 * (covar[1:2, :] + default_base),
@@ -185,48 +186,48 @@
         ],
         axis=0,
     )
+    share_n = n // n_paths
+    for q in range(n_paths):
+        loan_tx[q] = bundle[:, q * share_n:(q + 1) * share_n]
     pl.semaphore_wait(barrier, n_loans + n_paths - 2)
-    loan_copies, hpi_copies, end_copies = [], [], []
+    loan_copies, pass_copies, hpi_copies = [], [], [[] for _ in range(spans)]
     for off in range(1, n_loans):
-        there = lax.rem(me + off, n_loans)
+        there, source = lax.rem(me + off, n_loans), lax.rem(me + n_loans - off, n_loans)
         loan_copies.append(pltpu.make_async_remote_copy(
-            src_ref=loan_tx, dst_ref=loan_rx.at[me], send_sem=loan_ss.at[off], recv_sem=loan_rs.at[off],
-            device_id={"loans": there}, device_id_type=MESH))
-        hpi_copies.append(pltpu.make_async_remote_copy(
-            src_ref=hpi_tx.at[there], dst_ref=hpi_rx.at[me], send_sem=hpi_ss.at[off], recv_sem=hpi_rs.at[off],
-            device_id={"loans": there}, device_id_type=MESH))
-        end_copies.append(pltpu.make_async_remote_copy(
-            src_ref=end_tx.at[there], dst_ref=end_rx.at[me], send_sem=end_ss.at[off], recv_sem=end_rs.at[off],
-            device_id={"loans": there}, device_id_type=MESH))
+            src_ref=loan_tx.at[me_path], dst_ref=loan_rx.at[me, me_path], send_sem=loan_ss.at[off],
+            recv_sem=loan_rs.at[off], device_id={"loans": there}, device_id_type=MESH))
+        for hop in range(1, n_paths):
+            pass_copies.append(pltpu.make_async_remote_copy(
+                src_ref=loan_rx.at[source, me_path], dst_ref=loan_rx.at[source, me_path],
+                send_sem=pass_ss.at[off, hop], recv_sem=pass_rs.at[off, hop],
+                device_id={"paths": lax.rem(me_path + hop, n_paths)}, device_id_type=MESH))
+        for p in range(spans):
+            hpi_copies[p].append(pltpu.make_async_remote_copy(
+                src_ref=hpi_tx.at[p, there], dst_ref=hpi_rx.at[p, me], send_sem=hpi_ss.at[p, off],
+                recv_sem=hpi_rs.at[p, off], device_id={"loans": there}, device_id_type=MESH))
     for copy in loan_copies:
         copy.start()
-    own_loan = pltpu.make_async_copy(loan_tx, loan_rx.at[me], own_sem.at[0])
+    own_loan = pltpu.make_async_copy(loan_tx, loan_rx.at[me], own_sem.at[spans])
     own_loan.start()
-    blocks = [hpi[step] * (-0.5 * price_sens) for step in range(steps)]
-    quarter = lax.broadcasted_iota(jnp.int32, (rows, paths), 1) // here
-    for q in range(n_loans):
-        packs = None
-        for t in range(EARLY):
-            x = blocks[t] if t == q else pltpu.roll(blocks[t], ((t - q) % n_loans) * here, 1)
-            packs = x if packs is None else jnp.where(quarter == t, x, packs)
-        hpi_tx[q] = packs
-    for copy in hpi_copies:
-        copy.start()
-    own_hpi = pltpu.make_async_copy(hpi_tx.at[me], hpi_rx.at[me], own_sem.at[1])
-    own_hpi.start()
+    quarter = lax.broadcasted_iota(jnp.int32, (split, paths), 1) // here
     pad = jnp.zeros((2 * split - rows, paths), f32)
-    for q in range(n_loans):
-        packs = None
-        for t in range(n_loans):
-            x = blocks[EARLY + t % 2]
-            x = x[:split] if t < 2 else jnp.concatenate([x[split:], pad], axis=0)
-            x = x if t == q else pltpu.roll(x, ((t - q) % n_loans) * here, 1)
-            packs = x if packs is None else jnp.where(quarter[:split] == t, x, packs)
-        end_tx[q] = packs
-    for copy in end_copies:
-        copy.start()
-    own_end = pltpu.make_async_copy(end_tx.at[me], end_rx.at[me], own_sem.at[2])
-    own_end.start()
+    own_hpi = []
+    for p in range(spans):
+        blocks = []
+        for t in range(SPAN):
+            blocks.append(hpi[SPAN * p + t, 0:split, :] * (-0.5 * price_sens))
+        for t in range(SPAN):
+            blocks.append(jnp.concatenate([hpi[SPAN * p + t, split:rows, :] * (-0.5 * price_sens), pad], axis=0))
+        for q in range(n_loans):
+            packs = None
+            for t in range(n_loans):
+                x = blocks[t] if t == q else pltpu.roll(blocks[t], ((t - q) % n_loans) * here, 1)
+                packs = x if packs is None else jnp.where(quarter == t, x, packs)
+            hpi_tx[p, q] = packs
+        for copy in hpi_copies[p]:
+            copy.start()
+        own_hpi.append(pltpu.make_async_copy(hpi_tx.at[p, me], hpi_rx.at[p, me], own_sem.at[p]))
+        own_hpi[p].start()
 
     key = (jnp.broadcast_to(owner[...], (deals, deals)) * deals
            + lax.broadcasted_iota(jnp.int32, (deals, deals), 1)).astype(f32)
@@ -235,7 +236,6 @@
     spot = jnp.sum(below, axis=0, keepdims=True)
     perm = jnp.where(spot == lax.broadcasted_iota(jnp.int32, (deals, deals), 0).astype(f32), 1.0, 0.0).astype(f32)
     listing = jnp.sum(perm * lax.broadcasted_iota(jnp.int32, (deals, deals), 1).astype(f32), axis=1, keepdims=True)
-    listing = jnp.concatenate([listing] * copies, axis=0)
 
     def spread(x):
         x = jnp.dot(perm, x, preferred_element_type=f32, precision=lax.Precision.HIGHEST)
@@ -271,94 +271,70 @@
         disc.append(jnp.exp(-total / 12.0))
 
     own_loan.wait()
-    for copy in loan_copies:
+    for k, copy in enumerate(loan_copies):
+        copy.wait_recv()
+        for again in pass_copies[k * (n_paths - 1):(k + 1) * (n_paths - 1)]:
+            again.start()
+    for copy in pass_copies:
         copy.wait_recv()
     ages = lax.broadcasted_iota(jnp.int32, (8, n), 0).astype(f32)
+    depth = n_loans * wide
+    tail = SPAN * here
+    base_sums = jnp.zeros((32, lanes_out), f32)
     for src in range(n_loans):
-        r = loan_rx[src, 2:3, :]
+        lv = jnp.concatenate([loan_rx[src, q] for q in range(n_paths)], axis=1)
+        r = lv[2:3, :]
         grown = 1.0 + r
         log = jnp.log(grown) * (r / (grown - 1.0))
-        x = (loan_rx[src, 4:5, :] - ages) * log
+        x = (lv[4:5, :] - ages) * log
         left[src] = r / (jnp.exp(x) - 1.0)
-    pool[...] = jnp.zeros(pool.shape, f32)
-    own_hpi.wait()
-    for copy in hpi_copies:
-        copy.wait_recv()
-    height = EARLY * here
-    tail = (steps - EARLY) * here
-    for src in range(n_loans):
-        x = hpi_rx[src]
-        if wide > rows:
-            x = jnp.concatenate([x, jnp.zeros((wide - rows, paths), f32)], axis=0)
-        x = x.T
-        high = x.astype(bf16)
-        marks[0:height, src * wide:(src + 1) * wide] = high
-        marks[height:2 * height, src * wide:(src + 1) * wide] = (x - high.astype(f32)).astype(bf16)
-
-    depth = n_loans * wide
-
-    def months(got, held, lv, sched_rate, first, last, size):
-        r = lv[2:3, :]
-        for t in range(first, last):
-            k = t - first
-            h = got[k * here:(k + 1) * here] + got[size + k * here:size + (k + 1) * here]
-            smm = 0.5 + 0.5 * jnp.tanh(lv[0:1, :] - mort[t])
-            mdr = 0.5 + 0.5 * jnp.tanh(lv[1:2, :] + h)
-            interest = held * r
-            sched = held * sched_rate[t:t + 1, :]
-            lost = mdr * held
-            principal = sched + smm * (held - sched - lost) + lost
-            held = held - principal
-            base = k * 4 * here
-            for k, x in enumerate((principal, interest)):
-                high = x.astype(bf16)
-                cash[base + k * here:base + (k + 1) * here, :] = high
-                cash[base + (k + 2) * here:base + (k + 3) * here, :] = (x - high.astype(f32)).astype(bf16)
-        return held
-
-    def early(src, _):
-        lv = loan_rx[src]
-        pick = jnp.where(
+        picks[src] = jnp.where(
             lax.broadcasted_iota(jnp.int32, (depth, n), 0) == lv[5:6, :].astype(jnp.int32), 1.0, 0.0).astype(bf16)
-        picks[src] = pick
-        got = jnp.dot(marks[...], pick, preferred_element_type=f32)
-        held = months(got, jnp.broadcast_to(lv[3:4, :], (here, n)), lv, left[src], 0, EARLY, height)
-        balances[src] = held
+        hit = listing == lv[6:7, :]
+        r_high = r.astype(bf16).astype(f32)
+        member = jnp.concatenate(
+            [jnp.where(hit, 1.0, 0.0), jnp.where(hit, r_high, 0.0), jnp.where(hit, r - r_high, 0.0),
+             jnp.zeros((lanes_out - 3 * deals, n), f32)], axis=0).astype(bf16)
+        members[src] = member
         b = jnp.broadcast_to(lv[3:4, :], (16, n))
         high = b.astype(bf16)
-        cash[4 * height:4 * height + 16, :] = high
-        cash[4 * height + 16:4 * height + 32, :] = (b - high.astype(f32)).astype(bf16)
-        member = jnp.where(listing == lv[6:7, :], 1.0, 0.0).astype(bf16)
-        pool[0:4 * height + 32, :] += lax.dot_general(
-            cash[...], member, (((1,), (1,)), ((), ())), preferred_element_type=f32)
-        return 0
-
-    lax.fori_loop(0, n_loans, early, 0)
-
-    own_end.wait()
-    for copy in end_copies:
-        copy.wait_recv()
-    for src in range(n_loans):
-        x = jnp.concatenate([end_rx[src], jnp.zeros((128 - split, paths), f32)], axis=0).T
-        upper = pltpu.roll(x[tail:], split, 1)
-        x = jnp.where(lax.broadcasted_iota(jnp.int32, (tail, wide), 1) < split, x[:tail], upper)
-        high = x.astype(bf16)
-        end_marks[0:tail, src * wide:(src + 1) * wide] = high
-        end_marks[tail:2 * tail, src * wide:(src + 1) * wide] = (x - high.astype(f32)).astype(bf16)
-
-    def late(src, _):
-        lv = loan_rx[src]
-        got = jnp.dot(end_marks[...], picks[src], preferred_element_type=f32)
-        months(got, balances[src], lv, left[src], EARLY, steps, tail)
-        member = jnp.where(listing == lv[6:7, :], 1.0, 0.0).astype(bf16)
-        pool[4 * height + 32:, :] += lax.dot_general(
-            cash[0:4 * tail, :], member, (((1,), (1,)), ((), ())), preferred_element_type=f32)
-        return 0
-
-    lax.fori_loop(0, n_loans, late, 0)
-
-    start = pool[4 * height:4 * height + 1, :] + pool[4 * height + 16:4 * height + 17, :]
-    per_start = 1.0 / start
+        both = jnp.concatenate([high, (b - high.astype(f32)).astype(bf16)], axis=0)
+        base_sums = base_sums + lax.dot_general(both, member, (((1,), (1,)), ((), ())), preferred_element_type=f32)
+
+    for p in range(spans):
+        own_hpi[p].wait()
+        for copy in hpi_copies[p]:
+            copy.wait_recv()
+        for src in range(n_loans):
+            x = jnp.concatenate([hpi_rx[p, src], jnp.zeros((128 - split, paths), f32)], axis=0).T
+            upper = pltpu.roll(x[tail:], split, 1)
+            x = jnp.where(lax.broadcasted_iota(jnp.int32, (tail, wide), 1) < split, x[:tail], upper)
+            high = x.astype(bf16)
+            marks[p, 0:tail, src * wide:(src + 1) * wide] = high
+            marks[p, tail:2 * tail, src * wide:(src + 1) * wide] = (x - high.astype(f32)).astype(bf16)
+        sums = jnp.zeros((2 * tail, lanes_out), f32)
+        for src in range(n_loans):
+            lv = jnp.concatenate([loan_rx[src, q] for q in range(n_paths)], axis=1)
+            got = jnp.dot(marks[p], picks[src], preferred_element_type=f32)
+            held = jnp.broadcast_to(lv[3:4, :], (here, n)) if p == 0 else balances[src]
+            for t in range(SPAN):
+                h = got[t * here:(t + 1) * here] + got[tail + t * here:tail + (t + 1) * here]
+                smm = 0.5 + 0.5 * jnp.tanh(lv[0:1, :] - mort[SPAN * p + t])
+                mdr = 0.5 + 0.5 * jnp.tanh(lv[1:2, :] + h)
+                sched = held * left[src, SPAN * p + t:SPAN * p + t + 1, :]
+                lost = mdr * held
+                principal = sched + smm * (held - sched - lost) + lost
+                held = held - principal
+                high = principal.astype(bf16)
+                cash[src % 2, t * here:(t + 1) * here, :] = high
+                cash[src % 2, tail + t * here:tail + (t + 1) * here, :] = (
+                    principal - high.astype(f32)).astype(bf16)
+            if p < spans - 1:
+                balances[src] = held
+            sums = sums + lax.dot_general(
+                cash[src % 2], members[src], (((1,), (1,)), ((), ())), preferred_element_type=f32)
+        pool[p * tail:(p + 1) * tail, :] = sums[:tail] + sums[tail:]
+
     sub = here // copies
     group = lax.broadcasted_iota(jnp.int32, (sub, lanes_out), 1) // deals
 
@@ -369,15 +345,26 @@
             y = jnp.where(group == c, x[c * sub:(c + 1) * sub], y)
         return y
 
+    def shifted(x, column):
+        pieces = [x[c * sub:(c + 1) * sub] for c in range(copies)]
+        turned = [pltpu.roll(y, ((c - column) % copies) * deals, 1) if (c - column) % copies else y
+                  for c, y in enumerate(pieces)]
+        y = turned[0]
+        for c in range(1, copies):
+            y = jnp.where(group == c, turned[c], y)
+        return y
+
+    bases = jnp.concatenate([base_sums[0:sub] + base_sums[16:16 + sub]] * copies, axis=0)
+    per_start = 1.0 / shifted(bases, 0)
+    inter = shifted(bases, 1) + shifted(bases, 2)
     paid_upto = jnp.zeros((sub, lanes_out), f32)
     gone, gains, fall = [], [], []
     for t in range(steps):
-        base = t * 4 * here + (32 if t >= EARLY else 0)
-        princ = packed(pool[base:base + here, :] + pool[base + 2 * here:base + 3 * here, :])
-        inter = packed(pool[base + here:base + 2 * here, :] + pool[base + 3 * here:base + 4 * here, :])
-        paid_upto = paid_upto + jnp.maximum(princ, 0.0)
+        x = pool[t * here:(t + 1) * here, :]
+        paid_upto = paid_upto + jnp.maximum(shifted(x, 0), 0.0)
         gone.append(paid_upto * per_start)
         gains.append(inter * per_start)
+        inter = inter - (shifted(x, 1) + shifted(x, 2))
         fall.append(packed(disc[t]))
     worth = jnp.zeros((tranches, lanes_out), f32)
     for j in range(sub):
@@ -427,7 +414,7 @@
     acc = 100.0 * (acc / (paths * n_paths) - 1.0)
     out[:deals // 2, :] = acc[:, :tranches]
     out[deals // 2:, :] = pltpu.roll(acc, 64, 1)[:, :tranches]
-    for copy in loan_copies + hpi_copies + end_copies + part_copies + half_copies:
+    for copy in loan_copies + pass_copies + sum(hpi_copies, []) + part_copies + half_copies:
         copy.wait_send()
 
 
@@ -450,28 +437,26 @@
         in_specs=[pl.BlockSpec(memory_space=pltpu.VMEM)] * 14,
         out_specs=pl.BlockSpec(memory_space=pltpu.VMEM),
         scratch_shapes=[
-            pltpu.VMEM((8, n), f32),
+            pltpu.VMEM((n_paths, 8, n // n_paths), f32),
+            pltpu.VMEM((n_loans, n_paths, 8, n // n_paths), f32),
+            pltpu.VMEM((steps // SPAN, n_loans, split, paths), f32),
+            pltpu.VMEM((steps // SPAN, n_loans, split, paths), f32),
             pltpu.VMEM((n_loans, 8, n), f32),
-            pltpu.VMEM((n_loans, rows, paths), f32),
-            pltpu.VMEM((n_loans, rows, paths), f32),
-            pltpu.VMEM((n_loans, split, paths), f32),
-            pltpu.VMEM((n_loans, split, paths), f32),
-            pltpu.VMEM((n_loans, 8, n), f32),
-            pltpu.VMEM((2 * EARLY * here, n_loans * wide), jnp.bfloat16),
-            pltpu.VMEM((2 * (steps - EARLY) * here, n_loans * wide), jnp.bfloat16),
+            pltpu.VMEM((steps // SPAN, 2 * SPAN * here, n_loans * wide), jnp.bfloat16),
             pltpu.VMEM((n_loans, n_loans * wide, n), jnp.bfloat16),
+            pltpu.VMEM((n_loans, lanes_out, n), jnp.bfloat16),
             pltpu.VMEM((n_loans, here, n), f32),
-            pltpu.VMEM((4 * EARLY * here + 32, n), jnp.bfloat16),
-            pltpu.VMEM((4 * height + 32, lanes_out), f32),
+            pltpu.VMEM((2, 2 * SPAN * here, n), jnp.bfloat16),
+            pltpu.VMEM((height, lanes_out), f32),
             pltpu.VMEM((tranches, lanes_out), f32),
             pltpu.VMEM((paths, 128), f32),
             pltpu.VMEM((deals // 2, 128), f32),
             pltpu.VMEM((n_loans, deals // 2, 128), f32),
             pltpu.VMEM((deals // 2, 128), f32),
             pltpu.VMEM((n_paths, deals // 2, 128), f32),
-            dma((n_loans,)), dma((n_loans,)), dma((n_loans,)), dma((n_loans,)),
-            dma((n_loans,)), dma((n_loans,)), dma((n_loans,)), dma((n_loans,)),
-            dma((n_paths,)), dma((n_paths,)), dma((3,)),
+            dma((n_loans,)), dma((n_loans,)), dma((n_loans, n_paths)), dma((n_loans, n_paths)),
+            dma((steps // SPAN, n_loans)), dma((steps // SPAN, n_loans)),
+            dma((n_loans,)), dma((n_loans,)), dma((n_paths,)), dma((n_paths,)), dma((steps // SPAN + 1,)),
         ],
         compiler_params=pltpu.CompilerParams(collective_id=0, has_side_effects=True),
     )(loan_features, hazard_coef.T, rows_of(coupon), rows_of(balance), rows_of(loan_term), rows_of(loan_age),
@@ -486,9 +471,10 @@
     n_loans = lax.axis_size("loans")
     rows, steps = args[8].shape[:2]
     return (
-        paths == 128 and n_loans == EARLY and steps == EARLY + 2 and rows % 8 == 0 and 64 < rows <= 128
-        and deals % 16 == 0 and 128 % deals == 0 and tranches == 64
-        and (paths // n_loans) % (8 * (128 // deals)) == 0 and n % 128 == 0 and n <= 2048
+        paths == 128 and n_loans == 2 * SPAN and steps % SPAN == 0 and steps <= 8 and rows % 8 == 0 and 64 < rows <= 128
+        and deals in (16, 32) and tranches == 64
+        and (paths // n_loans) % (8 * (128 // deals)) == 0
+        and n % (128 * lax.axis_size("paths")) == 0 and n <= 2048
     )
 
 

time: 34.4 us -> 28.7 us (0.83)
  Pallas kernels: 32.8 us -> 27.2 us
    pallas_call x1, Pallas kernels: 32.8 us -> 27.2 us  [fused(): pl.pallas_call(functools.partial(pool_kernel, (n_loans, n_paths), lanes_o...]
where the time goes in v3:
time: 28.7 us; the launch traced here: 28.5 us
  Pallas kernels  27.2 us (95%)
  local copies, waits for them, and re-layouts  1.32 us (5%)
    pallas_call x1, Pallas kernels, fused(): pl.pallas_call(functools.partial(pool_kernel, (n_loans, n_paths), lanes_o...  27.2 us
    unnamed x1, local copies, waits for them, and re-layouts  1.32 us

profile of v3, /device:TPU:0, one launch (start us, length us, event | category | flops | bytes accessed | tf_op | source)
XLA Modules:
  0.0 28.5 jit_solution(5027632802178981623)
XLA Ops:
  0.0 27.2 %shard_map.136 = f32[32,64]{1,0:T(8,128)} custom-call(bf16[1024,128]{1,0:T(8,128)(2,1)} %feat.1, bf16[2,128]{1,0:T(2,128)(2,1)} %bitcast.18, f32[1,1024]{1,0:T(1,128)} %bitcast.12, f32[1,1024]{1,0:T(1,128)} %bitcast.13, s32[1,1024]{1,0:T(1,128)} %bitcast.14, s32[1,1024]{1,0:T(1,128)} %bitcast.15, s32[1,1024]{1,0:T(1,128)} %bitcast.16, s32[1,1024]{1,0:T(1,128)} %bitcast.17, ...), custom_call_target="tpu_custom_call" | custom-call | tf_op jit(solution)/shard_map/pallas_call | solution.py:434
  27.2 1.3 %copy.16 = f32[32,64]{1,0:T(8,128)} copy(f32[32,64]{1,0:T(8,128)} %shard_map.136) | data formatting | bytes 16384
